TPU v7x, 256 devices: a whole 4x4x8 slice. The times are simulated.
256 devices in a mesh: sect: 16 (over x, y), sec: 16 (over z, core).
Axes of the slice: x: 4, y: 4, z: 8, core: 2. Of those that a mesh axis runs over, the one named last changes fastest.
Arguments:
- psi_first: bfloat16 [16, 128, 128, 128], P('sect', 'sec'), may hold values from -100 to 100
- psi_second: bfloat16 [16, 128, 128, 128], P('sect', 'sec'), may hold values from -100 to 100
- left_env: bfloat16 [16, 14, 128, 128, 128], P('sect', None, 'sec'), may hold values from -1 to 2
- right_env: bfloat16 [16, 14, 128, 128, 128], P('sect', None, 'sec'), may hold values from -1 to 2
- couplings: float32 [16, 128, 4, 14], P('sect', 'sec'), may hold values from -2 to 3
- pair_sector: int32 [128, 4], P('sec'), may hold values from 0 to 127, as said below
Outputs:
- wave_first: bfloat16 [16, 128, 128, 128], P('sect', 'sec')
- wave_second: bfloat16 [16, 128, 128, 128], P('sect', 'sec')
- energies: float32 [16, 2], P('sect')
Inputs may be any that keep to these rules, and one draw needn't show every extreme that they name: `pair_sector`: A sector held at local position l of index d of sec (sector d * 8 + l) names only sectors o * 8 + ((d + k) mod 8) with 0 <= k < 2, for any o.
All inputs are finite; a program needn't handle non-finite values.
Results may differ from a plain program's by a relative error of at most 0.035.
Values may be sent and summed in bfloat16 or wider, within the bound.
A program may use at most 128 MiB of HBM per device.

v0:
```python
import jax
import jax.numpy as jnp
from jax import lax
from jax.sharding import PartitionSpec as P

BLK = 128
ITERS = 3


descent = 0.1


def shifted(value, axis, steps):
    count = lax.axis_size(axis)
    initial, last = (max(0, -steps), min(count, count - steps))
    return lax.ppermute(value, axis, [(source, source + steps) for source in range(initial, last)])


def fetch_blocks(wave_b, pairs):
    whole = lax.all_gather(wave_b, "sec", axis=0, tiled=True)
    return whole[pairs]


def hamiltonian(wave_b, left, right, coup, pairs):
    blocks = fetch_blocks(wave_b, pairs)
    mixed = jnp.einsum("sjm,sjab->msab", coup, blocks.astype(jnp.float32)).astype(jnp.bfloat16)
    inner = jnp.einsum("msab,msbc->msac", left, mixed, preferred_element_type=jnp.float32).astype(
        jnp.bfloat16
    )
    return jnp.einsum("msab,msbc->sac", inner, right, preferred_element_type=jnp.float32)


def bond_step(start, left, right, coup, pairs):
    state = start.astype(jnp.float32)
    total = lax.axis_size("sec") * state.shape[0] * state.shape[1] * state.shape[2]
    quot = jnp.float32(0.0)
    for step in range(ITERS):
        wave_b = state.astype(jnp.bfloat16)
        image = hamiltonian(wave_b, left, right, coup, pairs)
        flat = wave_b.astype(jnp.float32)
        norm_sq, numer = lax.psum((jnp.sum(flat * flat), jnp.sum(flat * image)), "sec")
        quot = numer / norm_sq
        fresh = flat - descent * (image - quot * flat)
        size_sq = lax.psum(jnp.sum(fresh * fresh), "sec")
        state = fresh * lax.rsqrt(size_sq / total)
    return (state.astype(jnp.bfloat16), quot)


def transport(wave_b, left):
    transit = jnp.einsum("msab,sbc->msac", left, wave_b, preferred_element_type=jnp.float32).astype(
        jnp.bfloat16
    )
    passed = jnp.einsum("sba,msbc->msac", wave_b, transit, preferred_element_type=jnp.float32)
    return (passed / BLK).astype(jnp.bfloat16)


def on_device(psi_first, psi_second, left_env, right_env, couplings, pair_sector):
    left = left_env[0]
    right = right_env[0]
    coup = couplings[0]
    wave_one, quot_one = bond_step(psi_first[0], left, right, coup, pair_sector)
    passed = transport(wave_one, left)
    arrived = shifted(passed, "sect", 1)
    used = jnp.where(lax.axis_index("sect") == 0, left, arrived)
    wave_two, quot_two = bond_step(psi_second[0], used, right, coup, pair_sector)
    energies = jnp.stack([quot_one, quot_two])[None, :]
    return (wave_one[None], wave_two[None], energies)


def solution(mesh):
    placed = (
        P("sect", "sec", None, None),
        P("sect", "sec", None, None),
        P("sect", None, "sec", None, None),
        P("sect", None, "sec", None, None),
        P("sect", "sec", None, None),
        P("sec", None),
    )
    return jax.shard_map(
        on_device,
        mesh=mesh,
        in_specs=placed,
        out_specs=(P("sect", "sec", None, None), P("sect", "sec", None, None), P("sect", None)),
        check_vma=False,
    )
```

profile of v0, /device:TPU:1, one launch (start us, length us, event | category | flops | bytes accessed | tf_op | source)
XLA Modules:
  0.0 718.9 jit_solution(11104340104167787000)
XLA Ops:
  8.8 5.9 copy.59
  14.7 41.5 %all-gather.17.cloned.1.call-done = bf16[1,128,128,128]{3,2,0,1:T(8,128)(2,1)} async-done(((bf16[1,8,128,128]{3,2,0,1:T(8,128)(2,1)}), bf16[1,128,128,128]{3,2,0,1:T(8,128)(2,1)}) %all-gather.17.cloned.1.call-update) | async-done | bytes 4194320 | tf_op jit(solution)/shard_map/all_gather | solution.py:20
  56.2 3.0 gather_fusion
  59.2 3.2 convert_bitcast_fusion.5
  62.4 7.3 %fusion.130 = (f32[]{:T(128)}, f32[]{:T(128)}, f32[8,128,128]{2,1,0:T(8,128)S(1)}) fusion(bf16[1,8,128,128]{3,2,1,0:T(8,128)(2,1)S(1)} %copy-done.6, bf16[14,8,128,128]{2,3,0,1:T(8,128)(2,1)} %copy.59, bf16[14,8,128,128]{3,0,2,1:T(8,128)(2,1)} %convert_bitcast_fusion.5, bf16[1,14,8,128,128]{4,3,2,1,0:T(8,128)(2,1)} %param.9), kind=kOutput, calls=%fused_computation.105 | convolution fusion | flops 942014464 | bytes 11796488 | tf_op jit(solution)/shard_map/msab,msbc->sac/dot_general | solution.py:30
  69.7 23.8 %all-reduce.5 = (f32[]{:T(128)}, f32[]{:T(128)}) all-reduce(f32[]{:T(128)} %get-tuple-element.14, f32[]{:T(128)} %get-tuple-element.13), channel_id=1, replica_groups=mesh['sect'=16,'sec'=16] {'sec'}, use_global_device_ids=true, to_apply=%region_1.0 | all-reduce | flops 2 | bytes 16 | tf_op jit(solution)/shard_map/psum | solution.py:41
  94.8 0.7 multiply_reduce_fusion.5
  95.6 26.0 %psum.128 = f32[]{:T(128)} all-reduce(f32[]{:T(128)} %multiply_reduce_fusion.5), channel_id=1, replica_groups=mesh['sect'=16,'sec'=16] {'sec'}, use_global_device_ids=true, to_apply=%region_5.0 | all-reduce | flops 1 | bytes 8 | tf_op jit(solution)/shard_map/psum | solution.py:44
  122.3 0.8 multiply_convert_fusion.6
  123.2 41.6 %all-gather.9.cloned.1.call-done = bf16[128,128,128]{2,1,0:T(8,128)(2,1)} async-done(((bf16[8,128,128]{2,1,0:T(8,128)(2,1)}), bf16[128,128,128]{2,1,0:T(8,128)(2,1)}) %all-gather.9.cloned.1.call-update) | async-done | bytes 4194320 | tf_op jit(solution)/shard_map/all_gather | solution.py:20
  164.7 2.9 gather_fusion.1
  167.7 3.2 convert_bitcast_fusion.4
  170.9 7.3 %fusion.114 = (f32[]{:T(128)}, f32[]{:T(128)}, f32[8,128,128]{2,1,0:T(8,128)S(1)}) fusion(bf16[8,128,128]{2,1,0:T(8,128)(2,1)S(1)} %copy-done.4, bf16[14,8,128,128]{2,3,0,1:T(8,128)(2,1)} %copy.59, bf16[14,8,128,128]{3,0,2,1:T(8,128)(2,1)} %convert_bitcast_fusion.4, bf16[1,14,8,128,128]{4,3,2,1,0:T(8,128)(2,1)} %param.9), kind=kOutput, calls=%fused_computation.89 | convolution fusion | flops 942014464 | bytes 11796488 | tf_op jit(solution)/shard_map/msab,msbc->sac/dot_general | solution.py:30
  178.2 23.8 %all-reduce.4 = (f32[]{:T(128)}, f32[]{:T(128)}) all-reduce(f32[]{:T(128)} %get-tuple-element.12, f32[]{:T(128)} %get-tuple-element.11), channel_id=1, replica_groups=mesh['sect'=16,'sec'=16] {'sec'}, use_global_device_ids=true, to_apply=%region_7.0 | all-reduce | flops 2 | bytes 16 | tf_op jit(solution)/shard_map/psum | solution.py:41
  204.1 26.0 %psum.131 = f32[]{:T(128)} all-reduce(f32[]{:T(128)} %multiply_reduce_fusion.4), channel_id=1, replica_groups=mesh['sect'=16,'sec'=16] {'sec'}, use_global_device_ids=true, to_apply=%region_11.0 | all-reduce | flops 1 | bytes 8 | tf_op jit(solution)/shard_map/psum | solution.py:44
  230.7 0.8 multiply_convert_fusion.5
  232.4 40.8 %all-gather.11.cloned.1.call-done = bf16[128,128,128]{2,1,0:T(8,128)(2,1)} async-done(((bf16[8,128,128]{2,1,0:T(8,128)(2,1)}), bf16[128,128,128]{2,1,0:T(8,128)(2,1)}) %all-gather.11.cloned.1.call-update) | async-done | bytes 4194320 | tf_op jit(solution)/shard_map/all_gather | solution.py:20
  273.2 2.9 gather_fusion.2
  276.2 3.3 convert_bitcast_fusion.3
  279.4 7.3 %fusion.118 = (f32[]{:T(128)}, f32[]{:T(128)}, f32[8,128,128]{2,1,0:T(8,128)S(1)}) fusion(bf16[8,128,128]{2,1,0:T(8,128)(2,1)S(1)} %copy-done.2, bf16[14,8,128,128]{2,3,0,1:T(8,128)(2,1)} %copy.59, bf16[14,8,128,128]{3,0,2,1:T(8,128)(2,1)} %convert_bitcast_fusion.3, bf16[1,14,8,128,128]{4,3,2,1,0:T(8,128)(2,1)} %param.9), kind=kOutput, calls=%fused_computation.93 | convolution fusion | flops 942014464 | bytes 11796488 | tf_op jit(solution)/shard_map/msab,msbc->sac/dot_general | solution.py:30
  286.7 24.8 %all-reduce.3 = (f32[]{:T(128)}, f32[]{:T(128)}) all-reduce(f32[]{:T(128)} %get-tuple-element.10, f32[]{:T(128)} %get-tuple-element.9), channel_id=1, replica_groups=mesh['sect'=16,'sec'=16] {'sec'}, use_global_device_ids=true, to_apply=%region_13.0 | all-reduce | flops 2 | bytes 16 | tf_op jit(solution)/shard_map/psum | solution.py:41
  312.9 0.7 multiply_reduce_fusion.3
  313.6 26.5 %psum.134 = f32[]{:T(128)} all-reduce(f32[]{:T(128)} %multiply_reduce_fusion.3), channel_id=1, replica_groups=mesh['sect'=16,'sec'=16] {'sec'}, use_global_device_ids=true, to_apply=%region_17.0 | all-reduce | flops 1 | bytes 8 | tf_op jit(solution)/shard_map/psum | solution.py:44
  341.0 6.1 fusion
  347.1 5.0 collective-permute-start
  352.1 5.9 copy.28
  358.0 2.9 gather_fusion.3
  361.0 3.2 convert_bitcast_fusion.2
  364.2 64.3 %collective-permute-done = bf16[14,8,128,128]{2,3,0,1:T(8,128)(2,1)} collective-permute-done((bf16[14,8,128,128]{2,3,0,1:T(8,128)(2,1)}, bf16[14,8,128,128]{2,3,0,1:T(8,128)(2,1)}, u32[]{:S(2)}, u32[]{:S(2)}) %collective-permute-start) | collective-permute-done | bytes 3670048 | tf_op jit(solution)/shard_map/ppermute | solution.py:16
  428.5 2.2 bitcast_select_fusion
  430.7 7.5 %fusion.134 = (f32[]{:T(128)}, f32[]{:T(128)}, f32[8,128,128]{2,1,0:T(8,128)S(1)}) fusion(bf16[1,8,128,128]{3,2,1,0:T(8,128)(2,1)S(1)} %copy-done.7, bf16[14,8,128,128]{2,3,0,1:T(8,128)(2,1)} %bitcast_select_fusion, bf16[14,8,128,128]{3,0,2,1:T(8,128)(2,1)} %convert_bitcast_fusion.2, bf16[1,14,8,128,128]{4,3,2,1,0:T(8,128)(2,1)} %param.9), kind=kOutput, calls=%fused_computation.109 | convolution fusion | flops 942014464 | bytes 11796488 | tf_op jit(solution)/shard_map/msab,msbc->sac/dot_general | solution.py:30
  438.2 25.0 %all-reduce.2 = (f32[]{:T(128)}, f32[]{:T(128)}) all-reduce(f32[]{:T(128)} %get-tuple-element.8, f32[]{:T(128)} %get-tuple-element.7), channel_id=1, replica_groups=mesh['sect'=16,'sec'=16] {'sec'}, use_global_device_ids=true, to_apply=%region_19.20 | all-reduce | flops 2 | bytes 16 | tf_op jit(solution)/shard_map/psum | solution.py:41
  465.3 24.4 %psum.137 = f32[]{:T(128)} all-reduce(f32[]{:T(128)} %multiply_reduce_fusion.2), channel_id=1, replica_groups=mesh['sect'=16,'sec'=16] {'sec'}, use_global_device_ids=true, to_apply=%region_23.24 | all-reduce | flops 1 | bytes 8 | tf_op jit(solution)/shard_map/psum | solution.py:44
  490.4 0.8 multiply_convert_fusion.3
  491.3 44.6 %all-gather.13.cloned.1.call-done = bf16[128,128,128]{2,1,0:T(8,128)(2,1)} async-done(((bf16[8,128,128]{2,1,0:T(8,128)(2,1)}), bf16[128,128,128]{2,1,0:T(8,128)(2,1)}) %all-gather.13.cloned.1.call-update) | async-done | bytes 4194320 | tf_op jit(solution)/shard_map/all_gather | solution.py:20
  535.9 2.9 gather_fusion.4
  538.8 3.2 convert_bitcast_fusion.1
  542.0 7.5 %fusion.122 = (f32[]{:T(128)}, f32[]{:T(128)}, f32[8,128,128]{2,1,0:T(8,128)S(1)}) fusion(bf16[8,128,128]{2,1,0:T(8,128)(2,1)S(1)} %copy-done.5, bf16[14,8,128,128]{2,3,0,1:T(8,128)(2,1)} %bitcast_select_fusion, bf16[14,8,128,128]{3,0,2,1:T(8,128)(2,1)} %convert_bitcast_fusion.1, bf16[1,14,8,128,128]{4,3,2,1,0:T(8,128)(2,1)} %param.9), kind=kOutput, calls=%fused_computation.97 | convolution fusion | flops 942014464 | bytes 11796488 | tf_op jit(solution)/shard_map/msab,msbc->sac/dot_general | solution.py:30
  549.5 23.8 %all-reduce.1 = (f32[]{:T(128)}, f32[]{:T(128)}) all-reduce(f32[]{:T(128)} %get-tuple-element.6, f32[]{:T(128)} %get-tuple-element.5), channel_id=1, replica_groups=mesh['sect'=16,'sec'=16] {'sec'}, use_global_device_ids=true, to_apply=%region_25.26 | all-reduce | flops 2 | bytes 16 | tf_op jit(solution)/shard_map/psum | solution.py:41
  575.4 26.0 %psum.140 = f32[]{:T(128)} all-reduce(f32[]{:T(128)} %multiply_reduce_fusion.1), channel_id=1, replica_groups=mesh['sect'=16,'sec'=16] {'sec'}, use_global_device_ids=true, to_apply=%region_29.30 | all-reduce | flops 1 | bytes 8 | tf_op jit(solution)/shard_map/psum | solution.py:44
  602.0 0.8 multiply_convert_fusion.2
  602.9 41.6 %all-gather.15.cloned.1.call-done = bf16[128,128,128]{2,1,0:T(8,128)(2,1)} async-done(((bf16[8,128,128]{2,1,0:T(8,128)(2,1)}), bf16[128,128,128]{2,1,0:T(8,128)(2,1)}) %all-gather.15.cloned.1.call-update) | async-done | bytes 4194320 | tf_op jit(solution)/shard_map/all_gather | solution.py:20
  644.5 2.9 gather_fusion.5
  647.5 3.2 convert_bitcast_fusion
  650.7 7.5 %fusion.126 = (f32[]{:T(128)}, f32[]{:T(128)}, f32[8,128,128]{2,1,0:T(8,128)S(1)}) fusion(bf16[8,128,128]{2,1,0:T(8,128)(2,1)S(1)} %copy-done.3, bf16[14,8,128,128]{2,3,0,1:T(8,128)(2,1)} %bitcast_select_fusion, bf16[14,8,128,128]{3,0,2,1:T(8,128)(2,1)} %convert_bitcast_fusion, bf16[1,14,8,128,128]{4,3,2,1,0:T(8,128)(2,1)} %param.9), kind=kOutput, calls=%fused_computation.101 | convolution fusion | flops 942014464 | bytes 11796488 | tf_op jit(solution)/shard_map/msab,msbc->sac/dot_general | solution.py:30
  658.1 23.8 %all-reduce = (f32[]{:T(128)}, f32[]{:T(128)}) all-reduce(f32[]{:T(128)} %get-tuple-element.4, f32[]{:T(128)} %get-tuple-element.3), channel_id=1, replica_groups=mesh['sect'=16,'sec'=16] {'sec'}, use_global_device_ids=true, to_apply=%region_31.32 | all-reduce | flops 2 | bytes 16 | tf_op jit(solution)/shard_map/psum | solution.py:41
  684.0 26.0 %psum.143 = f32[]{:T(128)} all-reduce(f32[]{:T(128)} %multiply_reduce_fusion), channel_id=1, replica_groups=mesh['sect'=16,'sec'=16] {'sec'}, use_global_device_ids=true, to_apply=%region_35.36 | all-reduce | flops 1 | bytes 8 | tf_op jit(solution)/shard_map/psum | solution.py:44
  710.7 0.8 fusion.137
  (41 shorter events, 6.3 us)
Async XLA Ops:
  7.2 52.0 %copy-start = (f32[1,8,4,14]{3,2,1,0:T(4,128)S(1)}, f32[1,8,4,14]{3,2,1,0:T(4,128)}, u32[]{:S(2)}) copy-start(f32[1,8,4,14]{3,2,1,0:T(4,128)} %param.10) | copy-start | bytes 5380
  7.2 49.0 %all-gather.17.cloned.1.call-start = ((), (), s32[]{:S(2)}) async-start(), calls=%async_computation.4 | async-start | bytes 4456448 | tf_op jit(solution)/shard_map/all_gather | solution.py:20
  7.9 156.8 %all-gather.9.cloned.1.call-start = ((), (), s32[]{:S(2)}) async-start(), calls=%async_computation | async-start | bytes 4456448 | tf_op jit(solution)/shard_map/all_gather | solution.py:20
  56.2 6.2 copy-start.6
  123.1 47.8 %copy-start.4 = (bf16[8,128,128]{2,1,0:T(8,128)(2,1)S(1)}, bf16[8,128,128]{2,1,0:T(8,128)(2,1)}, u32[]{:S(2)}) copy-start(bf16[8,128,128]{2,1,0:T(8,128)(2,1)} %multiply_convert_fusion.6) | copy-start | bytes 786436
  123.1 150.1 %all-gather.11.cloned.1.call-start = ((), (), s32[]{:S(2)}) async-start(), calls=%async_computation.1 | async-start | bytes 4456448 | tf_op jit(solution)/shard_map/all_gather | solution.py:20
  231.6 126.5 %all-gather.19.cloned.1.call-start = ((), (), s32[]{:S(2)}) async-start(), calls=%async_computation.5 | async-start | bytes 4456448 | tf_op jit(solution)/shard_map/all_gather | solution.py:20
  232.2 47.3 %copy-start.2 = (bf16[8,128,128]{2,1,0:T(8,128)(2,1)S(1)}, bf16[8,128,128]{2,1,0:T(8,128)(2,1)}, u32[]{:S(2)}) copy-start(bf16[8,128,128]{2,1,0:T(8,128)(2,1)} %multiply_convert_fusion.5) | copy-start | bytes 786436
  232.2 303.7 %all-gather.13.cloned.1.call-start = ((), (), s32[]{:S(2)}) async-start(), calls=%async_computation.2 | async-start | bytes 4456448 | tf_op jit(solution)/shard_map/all_gather | solution.py:20
  341.0 6.1 copy-start.8
  347.1 81.4 %collective-permute-start = (bf16[14,8,128,128]{2,3,0,1:T(8,128)(2,1)}, bf16[14,8,128,128]{2,3,0,1:T(8,128)(2,1)}, u32[]{:S(2)}, u32[]{:S(2)}) collective-permute-start(bf16[14,8,128,128]{2,3,0,1:T(8,128)(2,1)} %fusion), channel_id=1, source_target_pairs={{0,16},{16,32},{32,48},{48,64},{64,80},{80,96},{96,112},{112,128},... | collective-permute-start | bytes 11010056 | tf_op jit(solution)/shard_map/ppermute | solution.py:16
  361.0 67.5 %copy-start.1 = (bf16[1,14,8,128,128]{3,4,1,2,0:T(8,128)(2,1)S(1)}, bf16[1,14,8,128,128]{3,4,1,2,0:T(8,128)(2,1)}, u32[]{:S(2)}) copy-start(bf16[1,14,8,128,128]{3,4,1,2,0:T(8,128)(2,1)} %copy.28) | copy-start | bytes 11010052
  364.2 66.5 %copy-start.7 = (bf16[1,8,128,128]{3,2,1,0:T(8,128)(2,1)S(1)}, bf16[1,8,128,128]{3,2,1,0:T(8,128)(2,1)}, u32[]{:S(2)}) copy-start(bf16[1,8,128,128]{3,2,1,0:T(8,128)(2,1)} %param.7) | copy-start | bytes 786436
  491.2 50.8 %copy-start.5 = (bf16[8,128,128]{2,1,0:T(8,128)(2,1)S(1)}, bf16[8,128,128]{2,1,0:T(8,128)(2,1)}, u32[]{:S(2)}) copy-start(bf16[8,128,128]{2,1,0:T(8,128)(2,1)} %multiply_convert_fusion.3) | copy-start | bytes 786436
  491.2 153.3 %all-gather.15.cloned.1.call-start = ((), (), s32[]{:S(2)}) async-start(), calls=%async_computation.3 | async-start | bytes 4456448 | tf_op jit(solution)/shard_map/all_gather | solution.py:20
  602.9 47.8 %copy-start.3 = (bf16[8,128,128]{2,1,0:T(8,128)(2,1)S(1)}, bf16[8,128,128]{2,1,0:T(8,128)(2,1)}, u32[]{:S(2)}) copy-start(bf16[8,128,128]{2,1,0:T(8,128)(2,1)} %multiply_convert_fusion.2) | copy-start | bytes 786436
Sparse Core Ops, SparseCore 0:
  9.8 46.3 all-gather.16
  123.2 41.4 all-gather.8
  231.7 41.4 all-gather.10
  274.9 40.5 all-gather.18
  491.3 44.4 all-gather.12
  603.0 41.4 all-gather.14
where the time goes:
time: 720 us; the launch traced here: 719 us
  blocking collectives  300 us (42%)
  waiting for transfers between devices  276 us (38%)
  matrix products  69.8 us (10%)
  local copies, waits for them, and re-layouts  29.7 us (4%)
  between operations  26.4 us (4%)
  other arithmetic  12.2 us (2%)
    all_gather x6, waiting for transfers between devices, fetch_blocks(): whole = lax.all_gather(wave_b, 'sec', axis=0, tiled=True)  210 us
    psum x6, blocking collectives, bond_step(): size_sq = lax.psum(jnp.sum(fresh * fresh), 'sec')  155 us
    psum x6, blocking collectives, bond_step(): lax.psum((jnp.sum(flat * flat), jnp.sum(flat * image)), 'sec')  145 us
    ppermute x1, waiting for transfers between devices, shifted(): lax.ppermute(value, axis, [(source, source + steps) for source in range(i...  64.3 us
    dot_general x6, matrix products, hamiltonian(): jnp.einsum('msab,msbc->sac', inner, right, preferred_element_type=jnp.flo...  44.3 us
    dot_general x6, matrix products, hamiltonian(): jnp.einsum('sjm,sjab->msab', coup, blocks.astype(jnp.float32))  19.4 us
    gather x6, local copies, waits for them, and re-layouts, fetch_blocks(): return whole[pairs]  17.6 us
  transfers between devices with their start and end apart: 7, of which 6 were waited for; matrix products, arithmetic and copies ran while one was open for 5% of the time, Pallas kernels for 0%

commit v1 on v0

v1 whole, which is shorter than its diff:
```python
import functools

import jax
import jax.numpy as jnp
from jax import lax
from jax.experimental import pallas as pl
from jax.experimental.pallas import tpu as pltpu
from jax.sharding import PartitionSpec as P

MESH = pl.DeviceIdType.MESH
BLK = 128
ITERS = 3
DESCENT = 0.1
F32 = jnp.float32
BF16 = jnp.bfloat16


def fold(tile):
    return jnp.sum(tile.reshape(tile.shape[0] // 8, 8, tile.shape[1]), axis=0)


def kernel(
    n_sect,
    n_sec,
    coup,
    pairs,
    psi_one,
    psi_two,
    left,
    right,
    wave_one,
    wave_two,
    energies,
    env,
    renv,
    cand,
    come,
    own,
    sent,
    image,
    stat,
    stat_own,
    coef,
    prev_wave,
    load_sem,
    send_sem,
    recv_sem,
    stat_send,
    stat_recv,
    env_send,
    env_recv,
    hand_sem,
):
    sect = lax.axis_index("sect")
    me = lax.axis_index("sec")
    following = lax.rem(sect + 1, n_sect)
    previous = lax.rem(sect + n_sect - 1, n_sect)
    terms, held = left.shape[0], left.shape[1]
    half = n_sec // 2
    total = float(n_sec * held * BLK * BLK)

    barrier = pltpu.get_barrier_semaphore()

    def greet(step, _):
        peer = lax.rem(me + step, n_sec)
        pl.semaphore_signal(barrier, inc=1, device_id=(sect, peer), device_id_type=MESH)
        return 0

    lax.fori_loop(1, n_sec, greet, 0)
    pl.semaphore_signal(barrier, inc=1, device_id=(following, me), device_id_type=MESH)
    pl.semaphore_signal(barrier, inc=1, device_id=(previous, me), device_id_type=MESH)

    def place(source, target, number):
        return pltpu.make_async_copy(source, target, load_sem.at[number])

    first = lax.rem(me, held)
    second = lax.rem(me + 1, held)
    loads = [
        place(psi_one, own.at[0], 0),
        place(psi_one.at[first], come.at[0, 2 * me], 1),
        place(psi_one.at[second], come.at[0, 2 * me + 1], 2),
        place(left, env.at[0], 3),
        place(right, renv, 4),
        place(psi_two, own.at[1], 5),
        place(psi_two.at[first], come.at[3, 2 * me], 6),
        place(psi_two.at[second], come.at[3, 2 * me + 1], 7),
    ]
    for load in loads:
        load.start()
    pl.semaphore_wait(barrier, n_sec + 1)

    def send_block(source, number, kind, peer):
        pltpu.make_async_remote_copy(
            src_ref=source,
            dst_ref=come.at[number, 2 * me + kind],
            send_sem=send_sem.at[number],
            recv_sem=recv_sem.at[number],
            device_id=(sect, peer),
            device_id_type=MESH,
        ).start()

    def send_sector(source, number, step):
        @pl.when(step != 0)
        def _():
            send_block(source, number, 0, lax.rem(me + step, n_sec))

        send_block(source, number, 0, lax.rem(me + step + half, n_sec))

        @pl.when(step != 1)
        def _():
            send_block(source, number, 1, lax.rem(me + step + n_sec - 1, n_sec))

        send_block(source, number, 1, lax.rem(me + step + half - 1, n_sec))

    def send_start(source, number):
        def body(step, _):
            send_sector(source.at[lax.rem(me + step, held)], number, step)
            return 0

        lax.fori_loop(0, held, body, 0)

    send_start(psi_one, 0)

    def send_env(term, _):
        pltpu.make_async_remote_copy(
            src_ref=left.at[term],
            dst_ref=env.at[1, term],
            send_sem=env_send.at[term],
            recv_sem=env_recv.at[term],
            device_id=(following, me),
            device_id_type=MESH,
        ).start()
        return 0

    lax.fori_loop(0, terms, send_env, 0)

    blocks = pl.ds(0, 2 * n_sec - 2)

    def arrived(number):
        pltpu.make_async_copy(come.at[number, blocks], come.at[number, blocks], recv_sem.at[number]).wait()

    def left_here(number):
        pltpu.make_async_copy(come.at[number, blocks], come.at[number, blocks], send_sem.at[number]).wait()

    for load in loads:
        load.wait()

    def begin(step):
        arrived(3 * step)

        def body(slot, _):
            cand[slot] = come[3 * step, slot]
            return 0

        lax.fori_loop(0, 2 * n_sec, body, 0, unroll=2)
        coef[2] = jnp.zeros((8, BLK), F32)

    def iterate(index, _):
        step = lax.div(index, ITERS)
        turn = lax.rem(index, ITERS)
        number = index + 1

        @pl.when(turn == 0)
        def _():
            begin(step)

        @pl.when(index == ITERS - 1)
        def _():
            send_start(psi_two, 3)

        shift = coef[2, 0:1, :]

        def sector(turned, sums):
            local = lax.rem(me + turned, held)
            slots = []
            for pair in range(4):
                name = pairs[local * 4 + pair]
                slots.append(2 * lax.div(name, held) + lax.rem(name + n_sec - me, held))
            total_image = jnp.zeros((BLK, BLK), F32)
            for term in range(terms):
                mixed = None
                for pair in range(4):
                    part = coup[(local * 4 + pair) * terms + term] * cand[slots[pair]].astype(F32)
                    mixed = part if mixed is None else mixed + part
                inner = jnp.dot(env[step, term, local], mixed.astype(BF16), preferred_element_type=F32)
                total_image = total_image + jnp.dot(
                    inner.astype(BF16), renv[term, local], preferred_element_type=F32
                )
            mine = own[step, local].astype(F32)
            rest = total_image - shift * mine

            @pl.when(turn < ITERS - 1)
            def _():
                sent[index, local] = rest.astype(BF16)

                @pl.when(turned < 2)
                def _():
                    come[number, 2 * me + turned] = rest.astype(BF16)

                send_sector(sent.at[index, local], number, turned)

            @pl.when(turn == ITERS - 1)
            def _():
                image[local] = rest

            square, cross, rests = sums
            return (square + fold(mine * mine), cross + fold(mine * rest), rests + fold(rest * rest))

        zero = jnp.zeros((8, BLK), F32)
        square, cross, rests = lax.fori_loop(0, held, sector, (zero, zero, zero))
        stat_own[index, 0] = square
        stat_own[index, 1] = cross
        stat_own[index, 2] = rests
        stat[index, me] = stat_own[index]

        def tell(offset, _):
            pltpu.make_async_remote_copy(
                src_ref=stat_own.at[index],
                dst_ref=stat.at[index, me],
                send_sem=stat_send.at[index],
                recv_sem=stat_recv.at[index],
                device_id=(sect, lax.rem(me + offset, n_sec)),
                device_id_type=MESH,
            ).start()
            return 0

        lax.fori_loop(1, n_sec, tell, 0)
        others = pl.ds(0, n_sec - 1)
        pltpu.make_async_copy(stat.at[index, others], stat.at[index, others], stat_recv.at[index]).wait()
        sums = [jnp.sum(stat[index, :, kind], axis=0) for kind in range(3)]
        square, cross, rests = [
            jnp.broadcast_to(jnp.sum(value, axis=(0, 1), keepdims=True), (8, BLK)) for value in sums
        ]
        ratio = cross / square
        keep = 1.0 + DESCENT * ratio
        size = keep * keep * square - (2.0 * DESCENT) * keep * cross + (DESCENT * DESCENT) * rests
        scale = lax.rsqrt(size / total)
        coef[0] = keep * scale
        coef[1] = DESCENT * scale
        quot = coef[2] + ratio
        coef[2] = quot

        @pl.when(turn < ITERS - 1)
        def _():
            grow = coef[0, 0:1, :]
            drop = coef[1, 0:1, :]

            def own_body(local, _):
                own[step, local] = (
                    grow * own[step, local].astype(F32) - drop * sent[index, local].astype(F32)
                ).astype(BF16)
                return 0

            lax.fori_loop(0, held, own_body, 0, unroll=2)
            arrived(number)

            def cand_body(slot, _):
                cand[slot] = (
                    grow * cand[slot].astype(F32) - drop * come[number, slot].astype(F32)
                ).astype(BF16)
                return 0

            lax.fori_loop(0, 2 * n_sec, cand_body, 0, unroll=2)

        def finish(wave):
            grow = coef[0, 0:1, :]
            drop = coef[1, 0:1, :]

            def body(local, _):
                wave[local] = (grow * own[step, local].astype(F32) - drop * image[local]).astype(BF16)
                return 0

            lax.fori_loop(0, held, body, 0, unroll=2)

        @pl.when(index == ITERS - 1)
        def _():
            finish(wave_one)
            energies[0:1, 0:1] = coef[2, 0:1, 0:1]
            hand = pltpu.make_async_remote_copy(
                src_ref=wave_one,
                dst_ref=prev_wave,
                send_sem=hand_sem.at[0],
                recv_sem=hand_sem.at[1],
                device_id=(following, me),
                device_id_type=MESH,
            )
            hand.start()

            def here(term, _):
                pltpu.make_async_copy(env.at[1, term], env.at[1, term], env_recv.at[term]).wait()
                return 0

            lax.fori_loop(0, terms, here, 0)
            hand.wait()

            @pl.when(sect != 0)
            def _():
                def transport(local, _):
                    wave = prev_wave[local]
                    turned = wave.astype(F32).T.astype(BF16)
                    for term in range(terms):
                        transit = jnp.dot(env[1, term, local], wave, preferred_element_type=F32)
                        passed = jnp.dot(turned, transit.astype(BF16), preferred_element_type=F32)
                        env[1, term, local] = (passed * (1.0 / BLK)).astype(BF16)
                    return 0

                lax.fori_loop(0, held, transport, 0)

            @pl.when(sect == 0)
            def _():
                def same(term, _):
                    env[1, term] = env[0, term]
                    return 0

                lax.fori_loop(0, terms, same, 0)

        @pl.when(index == 2 * ITERS - 1)
        def _():
            finish(wave_two)
            energies[0:1, 1:2] = coef[2, 0:1, 0:1]

        return 0

    lax.fori_loop(0, 2 * ITERS, iterate, 0)

    for number in (0, 1, 2, 3, 4, 5):
        left_here(number)

    def told(index, _):
        others = pl.ds(0, n_sec - 1)
        pltpu.make_async_copy(stat.at[index, others], stat.at[index, others], stat_send.at[index]).wait()
        return 0

    lax.fori_loop(0, 2 * ITERS, told, 0)

    def env_left(term, _):
        pltpu.make_async_copy(env.at[1, term], env.at[1, term], env_send.at[term]).wait()
        return 0

    lax.fori_loop(0, terms, env_left, 0)


def solution(mesh):
    n_sect, n_sec = mesh.shape["sect"], mesh.shape["sec"]
    wide = P("sect", "sec", None, None)
    deep = P("sect", None, "sec", None, None)

    def on_device(psi_first, psi_second, left_env, right_env, couplings, pair_sector):
        terms, held = left_env.shape[1], left_env.shape[2]
        block = (BLK, BLK)
        hbm = pl.BlockSpec(memory_space=pl.ANY)
        vmem = pl.BlockSpec(memory_space=pltpu.VMEM)
        smem = pl.BlockSpec(memory_space=pltpu.SMEM)
        dma = pltpu.SemaphoreType.DMA
        waves = jax.ShapeDtypeStruct((held,) + block, BF16)
        one, two, energy = pl.pallas_call(
            functools.partial(kernel, n_sect, n_sec),
            out_shape=(waves, waves, jax.ShapeDtypeStruct((1, 2), F32)),
            in_specs=[smem, smem, hbm, hbm, hbm, hbm],
            out_specs=(vmem, vmem, vmem),
            scratch_shapes=[
                pltpu.VMEM((2, terms, held) + block, BF16),
                pltpu.VMEM((terms, held) + block, BF16),
                pltpu.VMEM((2 * n_sec,) + block, BF16),
                pltpu.VMEM((6, 2 * n_sec) + block, BF16),
                pltpu.VMEM((2, held) + block, BF16),
                pltpu.VMEM((6, held) + block, BF16),
                pltpu.VMEM((held,) + block, F32),
                pltpu.VMEM((6, n_sec, 3, 8, BLK), F32),
                pltpu.VMEM((6, 3, 8, BLK), F32),
                pltpu.VMEM((3, 8, BLK), F32),
                pltpu.VMEM((held,) + block, BF16),
                dma((8,)),
                dma((6,)),
                dma((6,)),
                dma((6,)),
                dma((6,)),
                dma((terms,)),
                dma((terms,)),
                dma((2,)),
            ],
            compiler_params=pltpu.CompilerParams(
                collective_id=0, has_side_effects=True, vmem_limit_bytes=50 * 1024 * 1024
            ),
        )(
            couplings.reshape(-1),
            pair_sector.reshape(-1),
            psi_first[0],
            psi_second[0],
            left_env[0],
            right_env[0],
        )
        return (one[None], two[None], energy)

    return jax.shard_map(
        on_device,
        mesh=mesh,
        in_specs=(wide, wide, deep, deep, wide, P("sec", None)),
        out_specs=(wide, wide, P("sect", None)),
        check_vma=False,
    )
```

time: 720 us -> 220 us (0.31)
  blocking collectives: 300 us -> 0 us
  waiting for transfers between devices: 276 us -> 0 us
  Pallas kernels: 0 us -> 212 us
  matrix products: 69.8 us -> 0 us
  between operations: 26.4 us -> 0.64 us
  local copies, waits for them, and re-layouts: 29.7 us -> 5.49 us
  other arithmetic: 12.2 us -> 0 us
    psum x12 -> x0, blocking collectives: 300 us -> none  [the longest x6 155 us: bond_step(): size_sq = lax.psum(jnp.sum(fresh * fresh), 'sec')]
    pallas_call x0 -> x1, Pallas kernels: none -> 212 us  [on_device(): pl.pallas_call(functools.partial(kernel, n_sect, n_sec), out_shape=(waves...]
    all_gather x6 -> x0, waiting for transfers between devices: 210 us -> none  [fetch_blocks(): whole = lax.all_gather(wave_b, 'sec', axis=0, tiled=True)]
    dot_general x13 -> x0, matrix products: 69.8 us -> none  [the longest x6 44.3 us: hamiltonian(): jnp.einsum('msab,msbc->sac', inner, right, preferred_element_type=jnp.flo...]
    ppermute x1 -> x0, waiting for transfers between devices: 64.3 us -> none  [shifted(): lax.ppermute(value, axis, [(source, source + steps) for source in range(i...]
    gather x6 -> x0, local copies, waits for them, and re-layouts: 17.6 us -> none  [fetch_blocks(): return whole[pairs]]
  transfers between devices with their start and end apart: 7 -> 0, of which waited for: 6 -> 0; matrix products, arithmetic and copies ran while one was open for 5% -> 0% of each run, Pallas kernels for 0% -> 0%
where the time goes in v1:
time: 220 us; the launch traced here: 218 us
  Pallas kernels  212 us (96%)
  local copies, waits for them, and re-layouts  5.49 us (2%)
    pallas_call x1, Pallas kernels, on_device(): pl.pallas_call(functools.partial(kernel, n_sect, n_sec), out_shape=(waves...  212 us
    unnamed x8, local copies, waits for them, and re-layouts  4.58 us

profile of v1, /device:TPU:1, one launch (start us, length us, event | category | flops | bytes accessed | tf_op | source)
XLA Modules:
  0.0 217.9 jit_solution(11767385658540339570)
XLA Ops:
  0.6 0.8 reshape.12.coup
  1.5 0.8 copy.10
  2.2 0.1 reshape.13.pairs
  2.3 0.0 copy-start
  2.3 1.0 copy-done
  3.3 0.0 copy-start.1
  3.3 0.9 copy-done.1
  4.2 211.8 %shard_map.85 = (bf16[8,128,128]{2,1,0:T(8,128)(2,1)S(1)}, bf16[8,128,128]{2,1,0:T(8,128)(2,1)S(1)}, f32[1,2]{1,0:T(1,128)S(1)}) custom-call(f32[448]{0:T(512)S(1)} %reshape.12.coup, s32[32]{0:T(128)S(1)} %reshape.13.pairs, bf16[8,128,128]{2,1,0:T(8,128)(2,1)S(1)} %bitcast.6, bf16[8,128,128]{2,1,0:T(8,128)(2,1)S(1)} %bitcast.7, ...), custom_call_target="tpu_custom_call" | custom-call | tf_op jit(solution)/shard_map/pallas_call | solution.py:356
  216.0 0.7 copy.14
  216.7 0.7 copy.15
  217.4 0.5 copy.16
Async XLA Ops:
  2.3 1.0 copy-start
  3.3 0.9 copy-start.1

commit v2 on v1

--- a/solution.py
+++ b/solution.py
@@ -22,8 +22,8 @@
 def kernel(
     n_sect,
     n_sec,
-    coup,
-    pairs,
+    coup_in,
+    pairs_in,
     psi_one,
     psi_two,
     left,
@@ -42,9 +42,13 @@
     stat_own,
     coef,
     prev_wave,
+    prev_turned,
+    coup,
+    pairs,
     load_sem,
     send_sem,
     recv_sem,
+    relay_sem,
     stat_send,
     stat_recv,
     env_send,
@@ -56,7 +60,6 @@
     following = lax.rem(sect + 1, n_sect)
     previous = lax.rem(sect + n_sect - 1, n_sect)
     terms, held = left.shape[0], left.shape[1]
-    half = n_sec // 2
     total = float(n_sec * held * BLK * BLK)
 
     barrier = pltpu.get_barrier_semaphore()
@@ -79,6 +82,8 @@
         place(psi_one, own.at[0], 0),
         place(psi_one.at[first], come.at[0, 2 * me], 1),
         place(psi_one.at[second], come.at[0, 2 * me + 1], 2),
+        place(coup_in, coup, 8),
+        place(pairs_in, pairs, 9),
         place(left, env.at[0], 3),
         place(right, renv, 4),
         place(psi_two, own.at[1], 5),
@@ -89,28 +94,63 @@
         load.start()
     pl.semaphore_wait(barrier, n_sec + 1)
 
-    def send_block(source, number, kind, peer):
+    def send_block(source, number, owner, kind, peer, done):
         pltpu.make_async_remote_copy(
             src_ref=source,
-            dst_ref=come.at[number, 2 * me + kind],
+            dst_ref=come.at[number, 2 * owner + kind],
             send_sem=send_sem.at[number],
-            recv_sem=recv_sem.at[number],
+            recv_sem=done,
             device_id=(sect, peer),
             device_id_type=MESH,
         ).start()
 
     def send_sector(source, number, step):
+        @pl.when(step != 1)
+        def _():
+            ahead = lax.rem(step + held - 1, held)
+            send_block(source, number, me, 1, lax.rem(me + ahead, n_sec), relay_sem.at[number, ahead - 1])
+
         @pl.when(step != 0)
         def _():
-            send_block(source, number, 0, lax.rem(me + step, n_sec))
-
-        send_block(source, number, 0, lax.rem(me + step + half, n_sec))
-
-        @pl.when(step != 1)
-        def _():
-            send_block(source, number, 1, lax.rem(me + step + n_sec - 1, n_sec))
-
-        send_block(source, number, 1, lax.rem(me + step + half - 1, n_sec))
+            behind = held - step
+            send_block(
+                source, number, me, 0, lax.rem(me + n_sec - behind, n_sec), relay_sem.at[number, held - 2 + behind]
+            )
+
+        @pl.when(step == 0)
+        def _():
+            send_block(source, number, me, 1, lax.rem(me + n_sec - 1, n_sec), recv_sem.at[number])
+
+        @pl.when(step == 1)
+        def _():
+            send_block(source, number, me, 0, lax.rem(me + 1, n_sec), recv_sem.at[number])
+
+    def relay(number):
+        def landed(lane):
+            pltpu.make_async_copy(come.at[number, 0], come.at[number, 0], relay_sem.at[number, lane]).wait()
+
+        def body(step, _):
+            @pl.when(step != 1)
+            def _():
+                ahead = lax.rem(step + held - 1, held)
+                owner = lax.rem(me + n_sec - ahead, n_sec)
+                landed(ahead - 1)
+                send_block(
+                    come.at[number, 2 * owner + 1], number, owner, 0, lax.rem(me + 1, n_sec), recv_sem.at[number]
+                )
+
+            @pl.when(step != 0)
+            def _():
+                behind = held - step
+                owner = lax.rem(me + behind, n_sec)
+                landed(held - 2 + behind)
+                send_block(
+                    come.at[number, 2 * owner], number, owner, 1, lax.rem(me + n_sec - 1, n_sec), recv_sem.at[number]
+                )
+
+            return 0
+
+        lax.fori_loop(0, held, body, 0)
 
     def send_start(source, number):
         def body(step, _):
@@ -134,16 +174,19 @@
 
     lax.fori_loop(0, terms, send_env, 0)
 
+    lanes = lax.broadcasted_iota(jnp.int32, (1, BLK), 1)
     blocks = pl.ds(0, 2 * n_sec - 2)
+    relayed = pl.ds(0, 2 * held)
 
     def arrived(number):
-        pltpu.make_async_copy(come.at[number, blocks], come.at[number, blocks], recv_sem.at[number]).wait()
+        pltpu.make_async_copy(come.at[number, relayed], come.at[number, relayed], recv_sem.at[number]).wait()
 
     def left_here(number):
         pltpu.make_async_copy(come.at[number, blocks], come.at[number, blocks], send_sem.at[number]).wait()
 
     for load in loads:
         load.wait()
+    relay(0)
 
     def begin(step):
         arrived(3 * step)
@@ -174,13 +217,13 @@
             local = lax.rem(me + turned, held)
             slots = []
             for pair in range(4):
-                name = pairs[local * 4 + pair]
+                name = pairs[local, pair]
                 slots.append(2 * lax.div(name, held) + lax.rem(name + n_sec - me, held))
             total_image = jnp.zeros((BLK, BLK), F32)
             for term in range(terms):
                 mixed = None
                 for pair in range(4):
-                    part = coup[(local * 4 + pair) * terms + term] * cand[slots[pair]].astype(F32)
+                    part = coup[local, pair, term] * cand[slots[pair]].astype(F32)
                     mixed = part if mixed is None else mixed + part
                 inner = jnp.dot(env[step, term, local], mixed.astype(BF16), preferred_element_type=F32)
                 total_image = total_image + jnp.dot(
@@ -208,10 +251,12 @@
 
         zero = jnp.zeros((8, BLK), F32)
         square, cross, rests = lax.fori_loop(0, held, sector, (zero, zero, zero))
-        stat_own[index, 0] = square
-        stat_own[index, 1] = cross
-        stat_own[index, 2] = rests
-        stat[index, me] = stat_own[index]
+        row = None
+        for kind, value in enumerate((square, cross, rests)):
+            part = jnp.where(lanes == kind, jnp.sum(value, axis=(0, 1), keepdims=True), 0.0)
+            row = part if row is None else row + part
+        stat_own[index] = row
+        stat[index, me] = row
 
         def tell(offset, _):
             pltpu.make_async_remote_copy(
@@ -225,11 +270,17 @@
             return 0
 
         lax.fori_loop(1, n_sec, tell, 0)
+
+        @pl.when(turn < ITERS - 1)
+        def _():
+            relay(number)
+
         others = pl.ds(0, n_sec - 1)
         pltpu.make_async_copy(stat.at[index, others], stat.at[index, others], stat_recv.at[index]).wait()
-        sums = [jnp.sum(stat[index, :, kind], axis=0) for kind in range(3)]
+        table = jnp.sum(stat[index], axis=0)
         square, cross, rests = [
-            jnp.broadcast_to(jnp.sum(value, axis=(0, 1), keepdims=True), (8, BLK)) for value in sums
+            jnp.broadcast_to(jnp.sum(jnp.where(lanes == kind, table, 0.0), axis=1, keepdims=True), (8, BLK))
+            for kind in range(3)
         ]
         ratio = cross / square
         keep = 1.0 + DESCENT * ratio
@@ -286,33 +337,32 @@
             )
             hand.start()
 
-            def here(term, _):
+            relay(3)
+            hand.wait()
+
+            def turn_wave(local, _):
+                prev_turned[local] = prev_wave[local].astype(F32).T.astype(BF16)
+                return 0
+
+            lax.fori_loop(0, held, turn_wave, 0)
+
+            def transport(term, _):
                 pltpu.make_async_copy(env.at[1, term], env.at[1, term], env_recv.at[term]).wait()
+
+                @pl.when(sect != 0)
+                def _():
+                    for local in range(held):
+                        transit = jnp.dot(env[1, term, local], prev_wave[local], preferred_element_type=F32)
+                        passed = jnp.dot(prev_turned[local], transit.astype(BF16), preferred_element_type=F32)
+                        env[1, term, local] = (passed * (1.0 / BLK)).astype(BF16)
+
+                @pl.when(sect == 0)
+                def _():
+                    env[1, term] = env[0, term]
+
                 return 0
 
-            lax.fori_loop(0, terms, here, 0)
-            hand.wait()
-
-            @pl.when(sect != 0)
-            def _():
-                def transport(local, _):
-                    wave = prev_wave[local]
-                    turned = wave.astype(F32).T.astype(BF16)
-                    for term in range(terms):
-                        transit = jnp.dot(env[1, term, local], wave, preferred_element_type=F32)
-                        passed = jnp.dot(turned, transit.astype(BF16), preferred_element_type=F32)
-                        env[1, term, local] = (passed * (1.0 / BLK)).astype(BF16)
-                    return 0
-
-                lax.fori_loop(0, held, transport, 0)
-
-            @pl.when(sect == 0)
-            def _():
-                def same(term, _):
-                    env[1, term] = env[0, term]
-                    return 0
-
-                lax.fori_loop(0, terms, same, 0)
+            lax.fori_loop(0, terms, transport, 0)
 
         @pl.when(index == 2 * ITERS - 1)
         def _():
@@ -350,13 +400,12 @@
         block = (BLK, BLK)
         hbm = pl.BlockSpec(memory_space=pl.ANY)
         vmem = pl.BlockSpec(memory_space=pltpu.VMEM)
-        smem = pl.BlockSpec(memory_space=pltpu.SMEM)
         dma = pltpu.SemaphoreType.DMA
         waves = jax.ShapeDtypeStruct((held,) + block, BF16)
         one, two, energy = pl.pallas_call(
             functools.partial(kernel, n_sect, n_sec),
             out_shape=(waves, waves, jax.ShapeDtypeStruct((1, 2), F32)),
-            in_specs=[smem, smem, hbm, hbm, hbm, hbm],
+            in_specs=[hbm] * 6,
             out_specs=(vmem, vmem, vmem),
             scratch_shapes=[
                 pltpu.VMEM((2, terms, held) + block, BF16),
@@ -366,13 +415,17 @@
                 pltpu.VMEM((2, held) + block, BF16),
                 pltpu.VMEM((6, held) + block, BF16),
                 pltpu.VMEM((held,) + block, F32),
-                pltpu.VMEM((6, n_sec, 3, 8, BLK), F32),
-                pltpu.VMEM((6, 3, 8, BLK), F32),
+                pltpu.VMEM((6, n_sec, 1, BLK), F32),
+                pltpu.VMEM((6, 1, BLK), F32),
                 pltpu.VMEM((3, 8, BLK), F32),
                 pltpu.VMEM((held,) + block, BF16),
-                dma((8,)),
+                pltpu.VMEM((held,) + block, BF16),
+                pltpu.SMEM(couplings.shape[1:], F32),
+                pltpu.SMEM(pair_sector.shape, jnp.int32),
+                dma((10,)),
                 dma((6,)),
                 dma((6,)),
+                dma((6, 2 * held - 2)),
                 dma((6,)),
                 dma((6,)),
                 dma((terms,)),
@@ -383,8 +436,8 @@
                 collective_id=0, has_side_effects=True, vmem_limit_bytes=50 * 1024 * 1024
             ),
         )(
-            couplings.reshape(-1),
-            pair_sector.reshape(-1),
+            couplings[0],
+            pair_sector,
             psi_first[0],
             psi_second[0],
             left_env[0],

time: 220 us -> 154 us (0.70)
  Pallas kernels: 212 us -> 145 us
    pallas_call x1, Pallas kernels: 212 us -> 145 us  [on_device(): pl.pallas_call(functools.partial(kernel, n_sect, n_sec), out_shape=(waves...]
    unnamed x8 -> x10, local copies, waits for them, and re-layouts: 4.58 us -> 5.29 us
where the time goes in v2:
time: 154 us; the launch traced here: 151 us
  Pallas kernels  145 us (94%)
  local copies, waits for them, and re-layouts  5.29 us (3%)
    pallas_call x1, Pallas kernels, on_device(): pl.pallas_call(functools.partial(kernel, n_sect, n_sec), out_shape=(waves...  145 us
    unnamed x10, local copies, waits for them, and re-layouts  5.29 us

profile of v2, /device:TPU:1, one launch (start us, length us, event | category | flops | bytes accessed | tf_op | source)
XLA Modules:
  0.0 150.8 jit_solution(15804833807913085775)
XLA Ops:
  0.6 0.8 copy.9.pairs_in
  1.4 0.0 copy-start
  1.4 0.9 copy-done
  2.3 0.0 copy-start.1
  2.3 0.9 copy-done.1
  3.3 0.0 copy-start.2
  3.3 0.7 copy-done.2
  4.0 144.9 %shard_map.85 = (bf16[8,128,128]{2,1,0:T(8,128)(2,1)S(1)}, bf16[8,128,128]{2,1,0:T(8,128)(2,1)S(1)}, f32[1,2]{1,0:T(1,128)S(1)}) custom-call(f32[8,4,14]{2,1,0:T(4,128)S(1)} %bitcast.11, s32[8,4]{1,0:T(8,128)S(1)} %copy.9.pairs_in, bf16[8,128,128]{2,1,0:T(8,128)(2,1)S(1)} %bitcast.7, bf16[8,128,128]{2,1,0:T(8,128)(2,1)S(1)} %bitcast.8, ...), custom_call_target="tpu_custom_call" | custom-call | tf_op jit(solution)/shard_map/pallas_call | solution.py:405
  148.9 0.7 copy.13
  149.6 0.7 copy.14
  150.3 0.5 copy.15
Async XLA Ops:
  1.4 0.9 copy-start
  2.3 0.9 copy-start.1
  3.3 0.7 copy-start.2

commit v3 on v2

--- a/solution.py
+++ b/solution.py
@@ -20,6 +20,7 @@
 
 
 def kernel(
+    side,
     n_sect,
     n_sec,
     coup_in,
@@ -42,7 +43,8 @@
     stat_own,
     coef,
     prev_wave,
-    prev_turned,
+    hop_one,
+    hop_two,
     coup,
     pairs,
     load_sem,
@@ -53,13 +55,27 @@
     stat_recv,
     env_send,
     env_recv,
-    hand_sem,
+    hop_send,
+    hop_recv,
+    hand_send,
+    hand_recv,
 ):
     sect = lax.axis_index("sect")
     me = lax.axis_index("sec")
     following = lax.rem(sect + 1, n_sect)
     previous = lax.rem(sect + n_sect - 1, n_sect)
     terms, held = left.shape[0], left.shape[1]
+    round_terms = hop_one.shape[0]
+    near_terms = terms - round_terms
+    batches = env_send.shape[0]
+    column, row_at = lax.rem(sect, side), lax.div(sect, side)
+    below = row_at * side + lax.rem(column + side - 1, side)
+    above = row_at * side + lax.rem(column + 1, side)
+    turns = lax.div(lax.rem(column + side - 2, side), side - 1)
+    turned_from = lax.div(lax.rem(column + side - 1, side), side - 1)
+    hop_to = turns * lax.rem(row_at + 1, side) * side + (1 - turns) * below
+    hop_from = turned_from * (lax.rem(row_at + side - 1, side) * side + 1) + (1 - turned_from) * above
+    half = n_sec // 2
     total = float(n_sec * held * BLK * BLK)
 
     barrier = pltpu.get_barrier_semaphore()
@@ -70,8 +86,8 @@
         return 0
 
     lax.fori_loop(1, n_sec, greet, 0)
-    pl.semaphore_signal(barrier, inc=1, device_id=(following, me), device_id_type=MESH)
-    pl.semaphore_signal(barrier, inc=1, device_id=(previous, me), device_id_type=MESH)
+    for section in (following, previous, below, above, hop_to, hop_from):
+        pl.semaphore_signal(barrier, inc=1, device_id=(section, me), device_id_type=MESH)
 
     def place(source, target, number):
         return pltpu.make_async_copy(source, target, load_sem.at[number])
@@ -92,7 +108,7 @@
     ]
     for load in loads:
         load.start()
-    pl.semaphore_wait(barrier, n_sec + 1)
+    pl.semaphore_wait(barrier, n_sec + 5)
 
     def send_block(source, number, owner, kind, peer, done):
         pltpu.make_async_remote_copy(
@@ -125,7 +141,7 @@
         def _():
             send_block(source, number, me, 0, lax.rem(me + 1, n_sec), recv_sem.at[number])
 
-    def relay(number):
+    def relay(number, between=None):
         def landed(lane):
             pltpu.make_async_copy(come.at[number, 0], come.at[number, 0], relay_sem.at[number, lane]).wait()
 
@@ -148,6 +164,8 @@
                     come.at[number, 2 * owner], number, owner, 1, lax.rem(me + n_sec - 1, n_sec), recv_sem.at[number]
                 )
 
+            if between is not None:
+                pl.when(step == 1)(between)
             return 0
 
         lax.fori_loop(0, held, body, 0)
@@ -161,18 +179,34 @@
 
     send_start(psi_one, 0)
 
-    def send_env(term, _):
-        pltpu.make_async_remote_copy(
-            src_ref=left.at[term],
-            dst_ref=env.at[1, term],
-            send_sem=env_send.at[term],
-            recv_sem=env_recv.at[term],
+    def batch(number):
+        low = number * near_terms // batches
+        span = pl.ds(low, (number + 1) * near_terms // batches - low)
+        return pltpu.make_async_remote_copy(
+            src_ref=left.at[span],
+            dst_ref=env.at[1, span],
+            send_sem=env_send.at[number],
+            recv_sem=env_recv.at[number],
             device_id=(following, me),
             device_id_type=MESH,
-        ).start()
-        return 0
-
-    lax.fori_loop(0, terms, send_env, 0)
+        )
+
+    batch(0).start()
+    tail = pl.ds(near_terms, round_terms)
+
+    def hop(number, section):
+        source = (left.at[tail], hop_one, hop_two)[number]
+        target = (hop_one, hop_two, env.at[1, tail])[number]
+        return pltpu.make_async_remote_copy(
+            src_ref=source,
+            dst_ref=target,
+            send_sem=hop_send.at[number],
+            recv_sem=hop_recv.at[number],
+            device_id=(section, me),
+            device_id_type=MESH,
+        )
+
+    hop(0, below).start()
 
     lanes = lax.broadcasted_iota(jnp.int32, (1, BLK), 1)
     blocks = pl.ds(0, 2 * n_sec - 2)
@@ -187,6 +221,7 @@
     for load in loads:
         load.wait()
     relay(0)
+    batch(1).start()
 
     def begin(step):
         arrived(3 * step)
@@ -197,6 +232,16 @@
 
         lax.fori_loop(0, 2 * n_sec, body, 0, unroll=2)
         coef[2] = jnp.zeros((8, BLK), F32)
+
+    def hand(local):
+        return pltpu.make_async_remote_copy(
+            src_ref=wave_one.at[local],
+            dst_ref=prev_wave.at[local],
+            send_sem=hand_send,
+            recv_sem=hand_recv.at[local],
+            device_id=(following, me),
+            device_id_type=MESH,
+        )
 
     def iterate(index, _):
         step = lax.div(index, ITERS)
@@ -207,17 +252,38 @@
         def _():
             begin(step)
 
-        @pl.when(index == ITERS - 1)
-        def _():
-            send_start(psi_two, 3)
-
         shift = coef[2, 0:1, :]
+
+        @pl.when(index == ITERS)
+        def _():
+            for number in range(batches):
+                batch(number).wait_recv()
+            hop(2, hop_to).wait_recv()
 
         def sector(turned, sums):
             local = lax.rem(me + turned, held)
+
+            @pl.when(index == ITERS)
+            def _():
+                hand(local).wait_recv()
+
+                @pl.when(sect != 0)
+                def _():
+                    wave = prev_wave[local]
+                    flipped = wave.astype(F32).T.astype(BF16)
+                    for term in range(terms):
+                        transit = jnp.dot(env[1, term, local], wave, preferred_element_type=F32)
+                        passed = jnp.dot(flipped, transit.astype(BF16), preferred_element_type=F32)
+                        env[1, term, local] = (passed * (1.0 / BLK)).astype(BF16)
+
+                @pl.when(sect == 0)
+                def _():
+                    for term in range(terms):
+                        env[1, term, local] = env[0, term, local]
+
             slots = []
             for pair in range(4):
-                name = pairs[local, pair]
+                name = pairs[pair, local]
                 slots.append(2 * lax.div(name, held) + lax.rem(name + n_sec - me, held))
             total_image = jnp.zeros((BLK, BLK), F32)
             for term in range(terms):
@@ -258,7 +324,8 @@
         stat_own[index] = row
         stat[index, me] = row
 
-        def tell(offset, _):
+        def tell(order, _):
+            offset = half + (1 - 2 * lax.rem(order, 2)) * lax.div(order + 1, 2)
             pltpu.make_async_remote_copy(
                 src_ref=stat_own.at[index],
                 dst_ref=stat.at[index, me],
@@ -269,11 +336,32 @@
             ).start()
             return 0
 
-        lax.fori_loop(1, n_sec, tell, 0)
-
-        @pl.when(turn < ITERS - 1)
-        def _():
-            relay(number)
+        lax.fori_loop(0, n_sec - 1, tell, 0)
+
+        @pl.when(index == 0)
+        def _():
+            def pass_on():
+                hop(0, below).wait_recv()
+                hop(1, below).start()
+
+            relay(number, pass_on)
+            batch(2).start()
+
+        @pl.when(index == 1)
+        def _():
+            def pass_on():
+                hop(1, below).wait_recv()
+                hop(2, hop_to).start()
+
+            relay(number, pass_on)
+            batch(3).start()
+            send_start(psi_two, 3)
+
+        @pl.when(index >= ITERS)
+        def _():
+            @pl.when(turn < ITERS - 1)
+            def _():
+                relay(number)
 
         others = pl.ds(0, n_sec - 1)
         pltpu.make_async_copy(stat.at[index, others], stat.at[index, others], stat_recv.at[index]).wait()
@@ -313,60 +401,28 @@
 
             lax.fori_loop(0, 2 * n_sec, cand_body, 0, unroll=2)
 
-        def finish(wave):
+        def finish(wave, onward):
             grow = coef[0, 0:1, :]
             drop = coef[1, 0:1, :]
 
-            def body(local, _):
+            def body(turned, _):
+                local = lax.rem(me + turned, held)
                 wave[local] = (grow * own[step, local].astype(F32) - drop * image[local]).astype(BF16)
+                if onward:
+                    hand(local).start()
                 return 0
 
-            lax.fori_loop(0, held, body, 0, unroll=2)
+            lax.fori_loop(0, held, body, 0)
 
         @pl.when(index == ITERS - 1)
         def _():
-            finish(wave_one)
+            finish(wave_one, True)
             energies[0:1, 0:1] = coef[2, 0:1, 0:1]
-            hand = pltpu.make_async_remote_copy(
-                src_ref=wave_one,
-                dst_ref=prev_wave,
-                send_sem=hand_sem.at[0],
-                recv_sem=hand_sem.at[1],
-                device_id=(following, me),
-                device_id_type=MESH,
-            )
-            hand.start()
-
             relay(3)
-            hand.wait()
-
-            def turn_wave(local, _):
-                prev_turned[local] = prev_wave[local].astype(F32).T.astype(BF16)
-                return 0
-
-            lax.fori_loop(0, held, turn_wave, 0)
-
-            def transport(term, _):
-                pltpu.make_async_copy(env.at[1, term], env.at[1, term], env_recv.at[term]).wait()
-
-                @pl.when(sect != 0)
-                def _():
-                    for local in range(held):
-                        transit = jnp.dot(env[1, term, local], prev_wave[local], preferred_element_type=F32)
-                        passed = jnp.dot(prev_turned[local], transit.astype(BF16), preferred_element_type=F32)
-                        env[1, term, local] = (passed * (1.0 / BLK)).astype(BF16)
-
-                @pl.when(sect == 0)
-                def _():
-                    env[1, term] = env[0, term]
-
-                return 0
-
-            lax.fori_loop(0, terms, transport, 0)
 
         @pl.when(index == 2 * ITERS - 1)
         def _():
-            finish(wave_two)
+            finish(wave_two, False)
             energies[0:1, 1:2] = coef[2, 0:1, 0:1]
 
         return 0
@@ -383,27 +439,29 @@
 
     lax.fori_loop(0, 2 * ITERS, told, 0)
 
-    def env_left(term, _):
-        pltpu.make_async_copy(env.at[1, term], env.at[1, term], env_send.at[term]).wait()
-        return 0
-
-    lax.fori_loop(0, terms, env_left, 0)
+    for number in range(batches):
+        batch(number).wait_send()
+    for number, section in ((0, below), (1, below), (2, hop_to)):
+        hop(number, section).wait_send()
+    pltpu.make_async_copy(prev_wave, prev_wave, hand_send).wait()
 
 
 def solution(mesh):
     n_sect, n_sec = mesh.shape["sect"], mesh.shape["sec"]
+    side = int(round(n_sect**0.5))
     wide = P("sect", "sec", None, None)
     deep = P("sect", None, "sec", None, None)
 
     def on_device(psi_first, psi_second, left_env, right_env, couplings, pair_sector):
         terms, held = left_env.shape[1], left_env.shape[2]
         block = (BLK, BLK)
-        hbm = pl.BlockSpec(memory_space=pl.ANY)
+        hbm = pl.BlockSpec(memory_space=pltpu.HBM)
+        round_terms = terms * 3 // 14
         vmem = pl.BlockSpec(memory_space=pltpu.VMEM)
         dma = pltpu.SemaphoreType.DMA
         waves = jax.ShapeDtypeStruct((held,) + block, BF16)
         one, two, energy = pl.pallas_call(
-            functools.partial(kernel, n_sect, n_sec),
+            functools.partial(kernel, side, n_sect, n_sec),
             out_shape=(waves, waves, jax.ShapeDtypeStruct((1, 2), F32)),
             in_specs=[hbm] * 6,
             out_specs=(vmem, vmem, vmem),
@@ -419,25 +477,29 @@
                 pltpu.VMEM((6, 1, BLK), F32),
                 pltpu.VMEM((3, 8, BLK), F32),
                 pltpu.VMEM((held,) + block, BF16),
-                pltpu.VMEM((held,) + block, BF16),
+                pltpu.VMEM((round_terms, held) + block, BF16),
+                pltpu.VMEM((round_terms, held) + block, BF16),
                 pltpu.SMEM(couplings.shape[1:], F32),
-                pltpu.SMEM(pair_sector.shape, jnp.int32),
+                pltpu.SMEM(pair_sector.shape[::-1], jnp.int32),
                 dma((10,)),
                 dma((6,)),
                 dma((6,)),
                 dma((6, 2 * held - 2)),
                 dma((6,)),
                 dma((6,)),
-                dma((terms,)),
-                dma((terms,)),
-                dma((2,)),
+                dma((4,)),
+                dma((4,)),
+                dma((3,)),
+                dma((3,)),
+                dma,
+                dma((held,)),
             ],
             compiler_params=pltpu.CompilerParams(
-                collective_id=0, has_side_effects=True, vmem_limit_bytes=50 * 1024 * 1024
+                collective_id=0, has_side_effects=True, vmem_limit_bytes=60 * 1024 * 1024
             ),
         )(
             couplings[0],
-            pair_sector,
+            pair_sector.T,
             psi_first[0],
             psi_second[0],
             left_env[0],

time: 154 us -> 131 us (0.85); the launches traced: 151 us -> 130 us
  Pallas kernels: 145 us -> 125 us
    pallas_call x1, Pallas kernels: 145 us -> 125 us  [on_device(): pl.pallas_call(functools.partial(kernel, side, n_sect, n_sec), out_shape=...]
    unnamed x10 -> x3, local copies, waits for them, and re-layouts: 5.29 us -> 4.45 us
where the time goes in v3:
time: 131 us; the launch traced here: 130 us
  Pallas kernels  125 us (95%)
  local copies, waits for them, and re-layouts  4.45 us (3%)
    pallas_call x1, Pallas kernels, on_device(): pl.pallas_call(functools.partial(kernel, side, n_sect, n_sec), out_shape=...  125 us
    unnamed x3, local copies, waits for them, and re-layouts  4.45 us

profile of v3, /device:TPU:1, one launch (start us, length us, event | category | flops | bytes accessed | tf_op | source)
XLA Modules:
  0.0 130.4 jit_solution(4766732714465850186)
XLA Ops:
  0.6 125.3 %shard_map.85 = (bf16[8,128,128]{2,1,0:T(8,128)(2,1)}, bf16[8,128,128]{2,1,0:T(8,128)(2,1)}, f32[1,2]{1,0:T(1,128)}) custom-call(f32[8,4,14]{2,1,0:T(4,128)} %bitcast.14, s32[4,8]{1,0:T(4,128)} %bitcast.15, bf16[8,128,128]{2,1,0:T(8,128)(2,1)} %bitcast.10, bf16[8,128,128]{2,1,0:T(8,128)(2,1)} %bitcast.11, bf16[14,8,128,128]{3,2,1,0:T(8,128)(2,1)} %bitcast.8, ...), custom_call_target="tpu_custom_call" | custom-call | tf_op jit(solution)/shard_map/pallas_call | solution.py:463
  125.9 1.7 %copy.12 = bf16[1,8,128,128]{3,2,1,0:T(8,128)(2,1)} copy(bf16[1,8,128,128]{3,2,1,0:T(8,128)(2,1)} %bitcast.13) | data formatting | bytes 524288
  127.6 1.7 %copy.13 = bf16[1,8,128,128]{3,2,1,0:T(8,128)(2,1)} copy(bf16[1,8,128,128]{3,2,1,0:T(8,128)(2,1)} %bitcast.12) | data formatting | bytes 524288
  129.3 1.1 copy.14

commit v4 on v3

--- a/solution.py
+++ b/solution.py
@@ -42,6 +42,7 @@
     stat,
     stat_own,
     coef,
+    parts,
     prev_wave,
     hop_one,
     hop_two,
@@ -65,9 +66,7 @@
     following = lax.rem(sect + 1, n_sect)
     previous = lax.rem(sect + n_sect - 1, n_sect)
     terms, held = left.shape[0], left.shape[1]
-    round_terms = hop_one.shape[0]
-    near_terms = terms - round_terms
-    batches = env_send.shape[0]
+    near_terms = terms - hop_one.shape[0]
     column, row_at = lax.rem(sect, side), lax.div(sect, side)
     below = row_at * side + lax.rem(column + side - 1, side)
     above = row_at * side + lax.rem(column + 1, side)
@@ -77,6 +76,9 @@
     hop_from = turned_from * (lax.rem(row_at + side - 1, side) * side + 1) + (1 - turned_from) * above
     half = n_sec // 2
     total = float(n_sec * held * BLK * BLK)
+
+    def far_first(order):
+        return lax.rem(held + (1 - 2 * lax.rem(order, 2)) * lax.div(order + 1, 2), held)
 
     barrier = pltpu.get_barrier_semaphore()
 
@@ -145,7 +147,9 @@
         def landed(lane):
             pltpu.make_async_copy(come.at[number, 0], come.at[number, 0], relay_sem.at[number, lane]).wait()
 
-        def body(step, _):
+        def body(order, _):
+            step = far_first(order)
+
             @pl.when(step != 1)
             def _():
                 ahead = lax.rem(step + held - 1, held)
@@ -165,49 +169,54 @@
                 )
 
             if between is not None:
-                pl.when(step == 1)(between)
+                pl.when(order == 1)(between)
             return 0
 
         lax.fori_loop(0, held, body, 0)
 
-    def send_start(source, number):
-        def body(step, _):
+    def send_start(source, number, low, high):
+        def body(order, _):
+            step = far_first(order)
             send_sector(source.at[lax.rem(me + step, held)], number, step)
             return 0
 
-        lax.fori_loop(0, held, body, 0)
-
-    send_start(psi_one, 0)
-
-    def batch(number):
-        low = number * near_terms // batches
-        span = pl.ds(low, (number + 1) * near_terms // batches - low)
+        lax.fori_loop(low, high, body, 0)
+
+    send_start(psi_one, 0, 0, held)
+
+    def position(order):
+        return lax.rem(me + far_first(order), held)
+
+    near = pl.ds(0, near_terms)
+    tail = pl.ds(near_terms, terms - near_terms)
+
+    def near_env(order):
         return pltpu.make_async_remote_copy(
-            src_ref=left.at[span],
-            dst_ref=env.at[1, span],
-            send_sem=env_send.at[number],
-            recv_sem=env_recv.at[number],
+            src_ref=left.at[near, position(order)],
+            dst_ref=env.at[1, near, position(order)],
+            send_sem=env_send.at[order],
+            recv_sem=env_recv.at[order],
             device_id=(following, me),
             device_id_type=MESH,
         )
 
-    batch(0).start()
-    tail = pl.ds(near_terms, round_terms)
-
-    def hop(number, section):
-        source = (left.at[tail], hop_one, hop_two)[number]
-        target = (hop_one, hop_two, env.at[1, tail])[number]
+    def hop(number):
         return pltpu.make_async_remote_copy(
-            src_ref=source,
-            dst_ref=target,
+            src_ref=(left.at[tail], hop_one, hop_two)[number],
+            dst_ref=(hop_one, hop_two, env.at[1, tail])[number],
             send_sem=hop_send.at[number],
             recv_sem=hop_recv.at[number],
-            device_id=(section, me),
+            device_id=(hop_to if number == 2 else below, me),
             device_id_type=MESH,
         )
 
-    hop(0, below).start()
-
+    def pass_on(number):
+        hop(number).wait_recv()
+        hop(number + 1).start()
+
+    hop(0).start()
+    near_env(0).start()
+    near_env(1).start()
     lanes = lax.broadcasted_iota(jnp.int32, (1, BLK), 1)
     blocks = pl.ds(0, 2 * n_sec - 2)
     relayed = pl.ds(0, 2 * held)
@@ -221,7 +230,8 @@
     for load in loads:
         load.wait()
     relay(0)
-    batch(1).start()
+    near_env(2).start()
+    near_env(3).start()
 
     def begin(step):
         arrived(3 * step)
@@ -254,33 +264,7 @@
 
         shift = coef[2, 0:1, :]
 
-        @pl.when(index == ITERS)
-        def _():
-            for number in range(batches):
-                batch(number).wait_recv()
-            hop(2, hop_to).wait_recv()
-
-        def sector(turned, sums):
-            local = lax.rem(me + turned, held)
-
-            @pl.when(index == ITERS)
-            def _():
-                hand(local).wait_recv()
-
-                @pl.when(sect != 0)
-                def _():
-                    wave = prev_wave[local]
-                    flipped = wave.astype(F32).T.astype(BF16)
-                    for term in range(terms):
-                        transit = jnp.dot(env[1, term, local], wave, preferred_element_type=F32)
-                        passed = jnp.dot(flipped, transit.astype(BF16), preferred_element_type=F32)
-                        env[1, term, local] = (passed * (1.0 / BLK)).astype(BF16)
-
-                @pl.when(sect == 0)
-                def _():
-                    for term in range(terms):
-                        env[1, term, local] = env[0, term, local]
-
+        def products(local):
             slots = []
             for pair in range(4):
                 name = pairs[pair, local]
@@ -295,31 +279,74 @@
                 total_image = total_image + jnp.dot(
                     inner.astype(BF16), renv[term, local], preferred_element_type=F32
                 )
+            return total_image
+
+        def sector(order, sums):
+            turned = far_first(order)
+            local = lax.rem(me + turned, held)
+
+            @pl.when(index == ITERS)
+            def _():
+                hand(local).wait_recv()
+
+                near_env(order).wait_recv()
+
+                @pl.when(order == 0)
+                def _():
+                    hop(2).wait_recv()
+
+                @pl.when(sect != 0)
+                def _():
+                    wave = prev_wave[local]
+                    flipped = wave.astype(F32).T.astype(BF16)
+                    for term in range(terms):
+                        transit = jnp.dot(env[1, term, local], wave, preferred_element_type=F32)
+                        passed = jnp.dot(flipped, transit.astype(BF16), preferred_element_type=F32)
+                        env[1, term, local] = (passed * (1.0 / BLK)).astype(BF16)
+
+                @pl.when(sect == 0)
+                def _():
+                    for term in range(terms):
+                        env[1, term, local] = env[0, term, local]
+
+            total_image = products(local)
             mine = own[step, local].astype(F32)
             rest = total_image - shift * mine
 
-            @pl.when(turn < ITERS - 1)
+            sent[index, local] = rest.astype(BF16)
+
+            @pl.when(turned < 2)
             def _():
-                sent[index, local] = rest.astype(BF16)
-
-                @pl.when(turned < 2)
-                def _():
-                    come[number, 2 * me + turned] = rest.astype(BF16)
-
-                send_sector(sent.at[index, local], number, turned)
-
-            @pl.when(turn == ITERS - 1)
-            def _():
-                image[local] = rest
-
+                come[number, 2 * me + turned] = rest.astype(BF16)
+
+            send_sector(sent.at[index, local], number, turned)
             square, cross, rests = sums
             return (square + fold(mine * mine), cross + fold(mine * rest), rests + fold(rest * rest))
 
+        def last_sector(local, sums):
+            mine = own[step, local].astype(F32)
+            rest = products(local) - shift * mine
+            image[local] = rest
+            square, cross, rests = sums
+            return (square + fold(mine * mine), cross + fold(mine * rest), rests + fold(rest * rest))
+
         zero = jnp.zeros((8, BLK), F32)
-        square, cross, rests = lax.fori_loop(0, held, sector, (zero, zero, zero))
+
+        def total_up(body, unroll):
+            for kind, value in enumerate(lax.fori_loop(0, held, body, (zero, zero, zero), unroll=unroll)):
+                parts[kind] = value
+
+        @pl.when(turn < ITERS - 1)
+        def _():
+            total_up(sector, 1)
+
+        @pl.when(turn == ITERS - 1)
+        def _():
+            total_up(last_sector, 4)
+
         row = None
-        for kind, value in enumerate((square, cross, rests)):
-            part = jnp.where(lanes == kind, jnp.sum(value, axis=(0, 1), keepdims=True), 0.0)
+        for kind in range(3):
+            part = jnp.where(lanes == kind, jnp.sum(parts[kind], axis=(0, 1), keepdims=True), 0.0)
             row = part if row is None else row + part
         stat_own[index] = row
         stat[index, me] = row
@@ -340,22 +367,16 @@
 
         @pl.when(index == 0)
         def _():
-            def pass_on():
-                hop(0, below).wait_recv()
-                hop(1, below).start()
-
-            relay(number, pass_on)
-            batch(2).start()
+            relay(number, functools.partial(pass_on, 0))
+            near_env(4).start()
+            near_env(5).start()
 
         @pl.when(index == 1)
         def _():
-            def pass_on():
-                hop(1, below).wait_recv()
-                hop(2, hop_to).start()
-
-            relay(number, pass_on)
-            batch(3).start()
-            send_start(psi_two, 3)
+            relay(number, functools.partial(pass_on, 1))
+            near_env(6).start()
+            near_env(7).start()
+            send_start(psi_two, 3, 0, held)
 
         @pl.when(index >= ITERS)
         def _():
@@ -391,22 +412,35 @@
                 return 0
 
             lax.fori_loop(0, held, own_body, 0, unroll=2)
-            arrived(number)
-
-            def cand_body(slot, _):
+            def renew(slot):
                 cand[slot] = (
                     grow * cand[slot].astype(F32) - drop * come[number, slot].astype(F32)
                 ).astype(BF16)
+
+            renew(2 * me)
+            renew(2 * me + 1)
+
+            def direct(away, _):
+                renew(2 * lax.rem(me + n_sec - away, n_sec) + 1)
+                renew(2 * lax.rem(me + away, n_sec))
                 return 0
 
-            lax.fori_loop(0, 2 * n_sec, cand_body, 0, unroll=2)
+            lax.fori_loop(1, held, direct, 0)
+            arrived(number)
+
+            def relayed_on(away, _):
+                renew(2 * lax.rem(me + n_sec - away, n_sec))
+                renew(2 * lax.rem(me + away, n_sec) + 1)
+                return 0
+
+            lax.fori_loop(1, held + 1, relayed_on, 0)
 
         def finish(wave, onward):
             grow = coef[0, 0:1, :]
             drop = coef[1, 0:1, :]
 
-            def body(turned, _):
-                local = lax.rem(me + turned, held)
+            def body(order, _):
+                local = lax.rem(me + far_first(order), held)
                 wave[local] = (grow * own[step, local].astype(F32) - drop * image[local]).astype(BF16)
                 if onward:
                     hand(local).start()
@@ -439,10 +473,10 @@
 
     lax.fori_loop(0, 2 * ITERS, told, 0)
 
-    for number in range(batches):
-        batch(number).wait_send()
-    for number, section in ((0, below), (1, below), (2, hop_to)):
-        hop(number, section).wait_send()
+    for order in range(held):
+        near_env(order).wait_send()
+    for number in range(3):
+        hop(number).wait_send()
     pltpu.make_async_copy(prev_wave, prev_wave, hand_send).wait()
 
 
@@ -456,7 +490,7 @@
         terms, held = left_env.shape[1], left_env.shape[2]
         block = (BLK, BLK)
         hbm = pl.BlockSpec(memory_space=pltpu.HBM)
-        round_terms = terms * 3 // 14
+        far_terms = terms * 3 // 14
         vmem = pl.BlockSpec(memory_space=pltpu.VMEM)
         dma = pltpu.SemaphoreType.DMA
         waves = jax.ShapeDtypeStruct((held,) + block, BF16)
@@ -476,9 +510,10 @@
                 pltpu.VMEM((6, n_sec, 1, BLK), F32),
                 pltpu.VMEM((6, 1, BLK), F32),
                 pltpu.VMEM((3, 8, BLK), F32),
+                pltpu.VMEM((3, 8, BLK), F32),
                 pltpu.VMEM((held,) + block, BF16),
-                pltpu.VMEM((round_terms, held) + block, BF16),
-                pltpu.VMEM((round_terms, held) + block, BF16),
+                pltpu.VMEM((far_terms, held) + block, BF16),
+                pltpu.VMEM((far_terms, held) + block, BF16),
                 pltpu.SMEM(couplings.shape[1:], F32),
                 pltpu.SMEM(pair_sector.shape[::-1], jnp.int32),
                 dma((10,)),
@@ -487,15 +522,15 @@
                 dma((6, 2 * held - 2)),
                 dma((6,)),
                 dma((6,)),
-                dma((4,)),
-                dma((4,)),
+                dma((held,)),
+                dma((held,)),
                 dma((3,)),
                 dma((3,)),
                 dma,
                 dma((held,)),
             ],
             compiler_params=pltpu.CompilerParams(
-                collective_id=0, has_side_effects=True, vmem_limit_bytes=60 * 1024 * 1024
+                collective_id=0, has_side_effects=True, vmem_limit_bytes=213 * 256 * 1024
             ),
         )(
             couplings[0],

time: 131 us -> 124 us (0.947)
  Pallas kernels: 125 us -> 120 us
    pallas_call x1, Pallas kernels: 125 us -> 120 us  [on_device(): pl.pallas_call(functools.partial(kernel, side, n_sect, n_sec), out_shape=...]
    unnamed x3 -> x7, local copies, waits for them, and re-layouts: 4.45 us -> 3.31 us
where the time goes in v4:
time: 124 us
  Pallas kernels  120 us (97%)
  local copies, waits for them, and re-layouts  3.31 us (3%)
    pallas_call x1, Pallas kernels, on_device(): pl.pallas_call(functools.partial(kernel, side, n_sect, n_sec), out_shape=...  120 us
    unnamed x7, local copies, waits for them, and re-layouts  3.31 us

profile of v4, /device:TPU:1, one launch (start us, length us, event | category | flops | bytes accessed | tf_op | source)
XLA Modules:
  0.0 123.9 jit_solution(12387400611919633324)
XLA Ops:
  0.6 0.0 copy-start
  0.6 0.7 copy-done
  1.4 0.0 copy-start.1
  1.4 0.7 copy-done.1
  2.0 119.9 %shard_map.85 = (bf16[8,128,128]{2,1,0:T(8,128)(2,1)S(1)}, bf16[8,128,128]{2,1,0:T(8,128)(2,1)S(1)}, f32[1,2]{1,0:T(1,128)S(1)}) custom-call(f32[8,4,14]{2,1,0:T(4,128)S(1)} %bitcast.10, s32[4,8]{1,0:T(4,128)S(1)} %bitcast.11, bf16[8,128,128]{2,1,0:T(8,128)(2,1)} %bitcast.14, bf16[8,128,128]{2,1,0:T(8,128)(2,1)} %bitcast.15, ...), custom_call_target="tpu_custom_call" | custom-call | tf_op jit(solution)/shard_map/pallas_call | solution.py:497
  122.0 0.7 copy.12
  122.7 0.7 copy.13
  123.4 0.5 copy.14
Async XLA Ops:
  0.6 0.7 copy-start
  1.4 0.7 copy-start.1

commit v5 on v4

--- a/solution.py
+++ b/solution.py
@@ -143,7 +143,7 @@
         def _():
             send_block(source, number, me, 0, lax.rem(me + 1, n_sec), recv_sem.at[number])
 
-    def relay(number, between=None):
+    def relay(number, between=None, low=0, high=None):
         def landed(lane):
             pltpu.make_async_copy(come.at[number, 0], come.at[number, 0], relay_sem.at[number, lane]).wait()
 
@@ -172,7 +172,7 @@
                 pl.when(order == 1)(between)
             return 0
 
-        lax.fori_loop(0, held, body, 0)
+        lax.fori_loop(low, held if high is None else high, body, 0)
 
     def send_start(source, number, low, high):
         def body(order, _):
@@ -240,7 +240,7 @@
             cand[slot] = come[3 * step, slot]
             return 0
 
-        lax.fori_loop(0, 2 * n_sec, body, 0, unroll=2)
+        lax.fori_loop(0, 2 * n_sec, body, 0, unroll=8)
         coef[2] = jnp.zeros((8, BLK), F32)
 
     def hand(local):
@@ -365,18 +365,23 @@
 
         lax.fori_loop(0, n_sec - 1, tell, 0)
 
+        @pl.when(index == ITERS - 1)
+        def _():
+            relay(3, None, 0, 3)
+
         @pl.when(index == 0)
         def _():
             relay(number, functools.partial(pass_on, 0))
             near_env(4).start()
             near_env(5).start()
+            send_start(psi_two, 3, 0, 2)
 
         @pl.when(index == 1)
         def _():
             relay(number, functools.partial(pass_on, 1))
             near_env(6).start()
             near_env(7).start()
-            send_start(psi_two, 3, 0, held)
+            send_start(psi_two, 3, 2, held)
 
         @pl.when(index >= ITERS)
         def _():
@@ -411,7 +416,8 @@
                 ).astype(BF16)
                 return 0
 
-            lax.fori_loop(0, held, own_body, 0, unroll=2)
+            lax.fori_loop(0, held, own_body, 0, unroll=4)
+
             def renew(slot):
                 cand[slot] = (
                     grow * cand[slot].astype(F32) - drop * come[number, slot].astype(F32)
@@ -433,7 +439,7 @@
                 renew(2 * lax.rem(me + away, n_sec) + 1)
                 return 0
 
-            lax.fori_loop(1, held + 1, relayed_on, 0)
+            lax.fori_loop(1, held + 1, relayed_on, 0, unroll=4)
 
         def finish(wave, onward):
             grow = coef[0, 0:1, :]
@@ -446,13 +452,13 @@
                     hand(local).start()
                 return 0
 
-            lax.fori_loop(0, held, body, 0)
+            lax.fori_loop(0, held, body, 0, unroll=1 if onward else 4)
 
         @pl.when(index == ITERS - 1)
         def _():
             finish(wave_one, True)
             energies[0:1, 0:1] = coef[2, 0:1, 0:1]
-            relay(3)
+            relay(3, None, 3)
 
         @pl.when(index == 2 * ITERS - 1)
         def _():

time: 124 us -> 123 us (level)
  no operation moved by 1% of the time
where the time goes in v5:
time: 123 us
  Pallas kernels  119 us (97%)
  local copies, waits for them, and re-layouts  3.31 us (3%)
    pallas_call x1, Pallas kernels, on_device(): pl.pallas_call(functools.partial(kernel, side, n_sect, n_sec), out_shape=...  119 us
    unnamed x7, local copies, waits for them, and re-layouts  3.31 us

profile of v5, /device:TPU:1, one launch (start us, length us, event | category | flops | bytes accessed | tf_op | source)
XLA Modules:
  0.0 122.9 jit_solution(10141946284660564573)
XLA Ops:
  0.6 0.0 copy-start
  0.6 0.7 copy-done
  1.4 0.0 copy-start.1
  1.4 0.7 copy-done.1
  2.0 119.0 %shard_map.85 = (bf16[8,128,128]{2,1,0:T(8,128)(2,1)S(1)}, bf16[8,128,128]{2,1,0:T(8,128)(2,1)S(1)}, f32[1,2]{1,0:T(1,128)S(1)}) custom-call(f32[8,4,14]{2,1,0:T(4,128)S(1)} %bitcast.10, s32[4,8]{1,0:T(4,128)S(1)} %bitcast.11, bf16[8,128,128]{2,1,0:T(8,128)(2,1)} %bitcast.14, bf16[8,128,128]{2,1,0:T(8,128)(2,1)} %bitcast.15, ...), custom_call_target="tpu_custom_call" | custom-call | tf_op jit(solution)/shard_map/pallas_call | solution.py:503
  121.0 0.7 copy.12
  121.7 0.7 copy.13
  122.4 0.5 copy.14
Async XLA Ops:
  0.6 0.7 copy-start
  1.4 0.7 copy-start.1

commit v6 on v5

--- a/solution.py
+++ b/solution.py
@@ -381,7 +381,6 @@
             relay(number, functools.partial(pass_on, 1))
             near_env(6).start()
             near_env(7).start()
-            send_start(psi_two, 3, 2, held)
 
         @pl.when(index >= ITERS)
         def _():
@@ -432,6 +431,11 @@
                 return 0
 
             lax.fori_loop(1, held, direct, 0)
+
+            @pl.when(index == 1)
+            def _():
+                send_start(psi_two, 3, 2, held)
+
             arrived(number)
 
             def relayed_on(away, _):

time: 123 us -> 124 us (level)
  no operation moved by 1% of the time
where the time goes in v6:
time: 124 us; the launch traced here: 123 us
  Pallas kernels  119 us (96%)
  local copies, waits for them, and re-layouts  3.31 us (3%)
    pallas_call x1, Pallas kernels, on_device(): pl.pallas_call(functools.partial(kernel, side, n_sect, n_sec), out_shape=...  119 us
    unnamed x7, local copies, waits for them, and re-layouts  3.31 us

profile of v6, /device:TPU:1, one launch (start us, length us, event | category | flops | bytes accessed | tf_op | source)
XLA Modules:
  0.0 123.4 jit_solution(12344294274042777927)
XLA Ops:
  0.6 0.0 copy-start
  0.6 0.7 copy-done
  1.4 0.0 copy-start.1
  1.4 0.7 copy-done.1
  2.0 119.4 %shard_map.85 = (bf16[8,128,128]{2,1,0:T(8,128)(2,1)S(1)}, bf16[8,128,128]{2,1,0:T(8,128)(2,1)S(1)}, f32[1,2]{1,0:T(1,128)S(1)}) custom-call(f32[8,4,14]{2,1,0:T(4,128)S(1)} %bitcast.10, s32[4,8]{1,0:T(4,128)S(1)} %bitcast.11, bf16[8,128,128]{2,1,0:T(8,128)(2,1)} %bitcast.14, bf16[8,128,128]{2,1,0:T(8,128)(2,1)} %bitcast.15, ...), custom_call_target="tpu_custom_call" | custom-call | tf_op jit(solution)/shard_map/pallas_call | solution.py:507
  121.5 0.7 copy.12
  122.2 0.7 copy.13
  122.9 0.5 copy.14
Async XLA Ops:
  0.6 0.7 copy-start
  1.4 0.7 copy-start.1
